TPU v7x, 256 devices: a whole 4x4x8 slice. The times are simulated.
256 devices in a mesh: region: 4 (over y), shard: 64 (over x, z, core).
Axes of the slice: x: 4, y: 4, z: 8, core: 2. Of those that a mesh axis runs over, the one named last changes fastest.
Arguments:
- features: bfloat16 [65536, 1024], P(('region', 'shard')), may hold values from -6 to 6
- proj_weight: bfloat16 [1024, 1024], replicated, may hold values from -0.1875 to 0.1875
- proj_bias: float32 [1024], replicated, may hold values from -3 to 3
- self_weight: bfloat16 [1024, 1024], replicated, may hold values from -0.1875 to 0.1875
- nbr_weight: bfloat16 [1024, 1024], replicated, may hold values from -0.1875 to 0.1875
- out_bias: float32 [1024], replicated, may hold values from -3 to 3
- nbr_ids: int32 [65536, 8], P(('region', 'shard')), may hold values from 0 to 16383, as said below
- nbr_counts: int32 [65536, 8], P(('region', 'shard')), may hold values from 1 to 32
- live_slots: int32 [512], P(('region', 'shard')), may hold values from 1 to 8
- query_ids: int32 [16384], P(('region', 'shard')), may hold values from 0 to 255
- positive_ids: int32 [16384], P(('region', 'shard')), may hold values from 0 to 255
- neg_blocks: int32 [256, 4], P(('region', 'shard')), may hold values from 0 to 7, as said below
Outputs:
- embedding: bfloat16 [65536, 1024], P(('region', 'shard'))
- hinge_terms: float32 [16384, 4], P(('region', 'shard'))
Inputs may be any that keep to these rules, and one draw needn't show every extreme that they name: `nbr_ids`: entries index items of the item's own region. Of the 2048 neighbour slots of one device, at most 64 name items held by any one device, and exactly 64 name the items of one device. `neg_blocks`: entry g names block g % 2 of the device at the same shard index in region g // 2; never a block of the device's own region.
All inputs are finite; a program needn't handle non-finite values.
Results may differ from a plain program's by a relative error of at most 0.0036.
Values may be sent and summed in bfloat16 or wider, within the bound.
A program may use at most 128 MiB of HBM per device.

v0:
```python
import jax
import jax.numpy as jnp
from jax import lax
from jax.sharding import PartitionSpec as P

score_scale = 32.0
margin_value = 1.0
norm_eps = 1e-06


def body(
    features,
    proj_weight,
    proj_bias,
    self_weight,
    nbr_weight,
    out_bias,
    nbr_ids,
    nbr_counts,
    live_slots,
    query_ids,
    positive_ids,
    neg_blocks,
):
    item_dev = features.shape[0]
    hidden = proj_weight.shape[1]
    fanout = nbr_ids.shape[1]
    block_rows = item_dev // live_slots.shape[0]
    shards = lax.axis_size("shard")
    live_item = jnp.repeat(live_slots, block_rows, total_repeat_length=item_dev)
    slot_weight = jnp.where(
        jnp.arange(fanout, dtype=jnp.int32)[None, :] < live_item[:, None], nbr_counts, 0
    )
    weight_sum = jnp.sum(slot_weight.astype(jnp.float32), axis=1, keepdims=True)
    flat_ids = nbr_ids.reshape(-1)
    owners = flat_ids // item_dev
    local_row = flat_ids % item_dev
    slots = flat_ids.shape[0]
    capacity = max(2, 2 * slots // shards)
    onehot = (owners[:, None] == jnp.arange(shards, dtype=jnp.int32)[None, :]).astype(jnp.int32)
    before = jnp.cumsum(onehot, axis=0) - onehot
    slot_rank = jnp.take_along_axis(before, owners[:, None], axis=1)[:, 0]
    requests = jnp.zeros((shards, capacity), jnp.int32).at[owners, slot_rank].set(local_row)
    wanted = lax.all_to_all(requests, "shard", split_axis=0, concat_axis=0, tiled=True)
    outgoing = jnp.take(features, wanted, axis=0)
    incoming = lax.all_to_all(outgoing, "shard", split_axis=0, concat_axis=0, tiled=True)
    gathered = incoming[owners, slot_rank]
    slot_proj = jnp.maximum(
        jnp.dot(gathered, proj_weight, preferred_element_type=jnp.float32) + proj_bias, 0.0
    ).astype(jnp.bfloat16)
    slot_proj = slot_proj.reshape(item_dev, fanout, hidden)
    summed = jnp.einsum(
        "ik,ikh->ih",
        slot_weight.astype(jnp.bfloat16),
        slot_proj,
        preferred_element_type=jnp.float32,
    )
    aggregate = (summed / weight_sum).astype(jnp.bfloat16)
    activation = (
        jnp.dot(features, self_weight, preferred_element_type=jnp.float32)
        + jnp.dot(aggregate, nbr_weight, preferred_element_type=jnp.float32)
        + out_bias
    )
    activation = jnp.maximum(activation, 0.0)
    embedding = (
        activation * lax.rsqrt(jnp.mean(activation * activation, axis=-1, keepdims=True) + norm_eps)
    ).astype(jnp.bfloat16)
    query_emb = jnp.take(embedding, query_ids, axis=0)
    positive_emb = jnp.take(embedding, positive_ids, axis=0)
    neg_lists = neg_blocks[0]
    positive_score = (
        score_scale
        / hidden
        * jnp.sum(query_emb.astype(jnp.float32) * positive_emb.astype(jnp.float32), axis=-1)
    )
    start_value = jnp.zeros((query_emb.shape[0], neg_lists.shape[0]), jnp.float32)
    scores = (
        score_scale
        / hidden
        * jnp.dot(
            query_emb,
            lax.all_gather(embedding, "region", axis=0, tiled=True).T,
            preferred_element_type=jnp.float32,
        )
    )
    hinge_all = jnp.maximum(scores - positive_score[:, None] + margin_value, 0.0)
    block_mean = jnp.mean(hinge_all.reshape(query_emb.shape[0], -1, block_rows), axis=-1)
    pool_ids = jnp.int32(0) // block_rows + jnp.arange(block_mean.shape[1], dtype=jnp.int32)
    picked = jnp.where(
        neg_lists[None, :, None] == pool_ids[None, None, :], block_mean[:, None, :], 0.0
    )
    hinge_terms = start_value + jnp.sum(picked, axis=-1)
    return (embedding, hinge_terms)


def solution(mesh):
    in_specs = (
        P(("region", "shard"), None),
        P(),
        P(),
        P(),
        P(),
        P(),
        P(("region", "shard"), None),
        P(("region", "shard"), None),
        P(("region", "shard")),
        P(("region", "shard")),
        P(("region", "shard")),
        P(("region", "shard"), None),
    )
    out_specs = (P(("region", "shard"), None), P(("region", "shard"), None))
    return jax.shard_map(body, mesh=mesh, in_specs=in_specs, out_specs=out_specs, check_vma=False)
```

profile of v0, /device:TPU:1, one launch (start us, length us, event | category | flops | bytes accessed | tf_op | source)
XLA Modules:
  0.0 386.9 jit_solution(6796952247601897155)
XLA Ops:
  7.2 0.0 copy-start
  7.2 1.0 copy.39
  8.2 0.1 reshape.447
  8.3 0.1 reshape.449
  8.4 0.1 reshape.450
  8.5 0.1 reshape.446
  8.7 18.1 %reduce-window.14 = s32[64,16,128]{2,1,0:T(8,128)S(1)} reduce-window(s32[64,16,128]{2,1,0:T(8,128)S(1)} %fusion.15, s32[]{:T(128)} %constant.161.clone.1), window={size=1x1x128 pad=0_0x0_0x127_0}, to_apply=%region_0.1 | reduce-window | flops 16646144 | bytes 1048580 | tf_op jit(solution)/shard_map/reduce-window.3
  26.8 0.2 slice.37
  27.0 0.4 copy.48
  27.5 0.2 reduce-window.15
  27.6 0.2 broadcast_add_fusion
  28.0 0.2 fusion.13
  28.2 0.0 copy-start.5
  28.2 0.0 copy-start.1
  28.2 16.8 %gather_fusion.2 = s32[2048]{0:T(1024)S(1)} fusion(s32[2048,64]{0,1:T(8,128)S(1)} %fusion.13, s32[2048]{0:T(1024)S(1)} %bitcast.55), kind=kCustom, calls=%fused_computation.4 | custom fusion | bytes 32768 | tf_op jit(solution)/shard_map/jit(take_along_axis)/gather | solution.py:42
  45.0 0.1 shift-left_or_fusion
  45.1 0.1 and_reduce_fusion
  45.2 0.0 copy-done.5
  45.2 0.1 multiply_reduce_fusion.2
  45.3 8.1 %scatter_custom_fusion = s32[4096]{0:T(1024)S(1)} fusion(s32[2048]{0:T(1024)S(1)} %broadcast_select_fusion.3, s32[2048]{0:T(1024)S(1)} %get-tuple-element.18, s32[]{:T(128)} %constant.161.clone.1), kind=kCustom, calls=%fused_computation.69 | custom fusion | bytes 16388
  53.4 0.1 all_to_all.13
  53.4 22.1 %all_to_all.20 = s32[64,1,64]{2,1,0:T(1,128)S(1)} all-to-all(s32[64,1,64]{2,1,0:T(1,128)S(1)} %all_to_all.13), channel_id=1, replica_groups=mesh['region'=4,'shard'=64] {'shard'}, dimensions={0} | all-to-all | bytes 32768 | tf_op jit(solution)/shard_map/all_to_all | solution.py:44
  75.5 0.1 reshape.485
  75.6 0.0 copy-done.1
  75.7 18.3 %gather_fusion = bf16[4096,1024]{1,0:T(8,128)(2,1)} fusion(bf16[256,1024]{1,0:T(8,128)(2,1)S(1)} %copy-done.1, s32[4096]{0:T(1024)S(1)} %broadcast_clamp_fusion), kind=kCustom, calls=%fused_computation.2 | custom fusion | bytes 16793600 | tf_op jit(solution)/shard_map/jit(_take)/gather | solution.py:45
  93.9 7.3 %broadcast_select_fusion = bf16[64,64,1024]{2,1,0:T(8,128)(2,1)} fusion(bf16[64,64,1024]{2,1,0:T(8,128)(2,1)} %bitcast.56, pred[64,64]{1,0:T(8,128)(4,1)S(1)} %compare_and_fusion), kind=kLoop, calls=%fused_computation.7 | loop fusion | flops 4194304 | bytes 16781312 | tf_op jit(solution)/shard_map/jit(_take)/select_n | solution.py:45
  101.2 0.0 copy-start.4
  101.2 0.0 copy-start.3
  101.2 5.9 %all-to-all-start.1 = ((bf16[64,64,1024]{2,1,0:T(8,128)(2,1)}), bf16[64,64,1024]{2,1,0:T(8,128)(2,1)}, u32[]{:S(2)}, u32[]{:S(2)}) async-start(bf16[64,64,1024]{2,1,0:T(8,128)(2,1)} %broadcast_select_fusion), calls=%async_computation.1 | async-start | bytes 16777216 | tf_op jit(solution)/shard_map/all_to_all | solution.py:46
  107.1 0.2 all-gather.2.cloned.1.call-start
  107.4 0.0 copy-done.4
  107.4 0.6 fusion.32
  108.0 1.3 compare_select_fusion.12
  109.3 0.0 copy-done.3
  109.3 0.2 copy.46
  109.5 3.3 fusion.33
  112.8 180.1 %all-to-all-done.1 = bf16[64,64,1024]{2,1,0:T(8,128)(2,1)} async-done(((bf16[64,64,1024]{2,1,0:T(8,128)(2,1)}), bf16[64,64,1024]{2,1,0:T(8,128)(2,1)}, u32[]{:S(2)}, u32[]{:S(2)}) %all-to-all-start.1) | async-done | bytes 8388640 | tf_op jit(solution)/shard_map/all_to_all | solution.py:46
  292.9 0.0 copy-start.6
  292.9 40.8 %gather_fusion.1 = bf16[2048,1024]{1,0:T(8,128)(2,1)} fusion(bf16[64,64,1024]{2,1,0:T(8,128)(2,1)} %all-to-all-done.1, s32[2048]{0:T(1024)S(1)} %bitcast.54), kind=kCustom, calls=%fused_computation.3 | custom fusion | bytes 8404992 | tf_op jit(solution)/shard_map/gather | solution.py:47
  333.7 0.0 copy-done.6
  333.7 0.0 copy-start.2
  333.7 0.0 copy-start.7
  333.7 9.6 %fusion.1 = f32[256,1,1024]{2,1,0:T(1,128)} fusion(bf16[256,8,1]{1,2,0:T(2,128)(2,1)S(1)} %copy.46, f32[1024]{0:T(1024)S(1)} %copy-done.6, bf16[2048,1024]{1,0:T(8,128)(2,1)} %gather_fusion.1, bf16[1024,1024]{1,0:T(8,128)(2,1)} %param.17), kind=kOutput, calls=%fused_computation.9 | convolution fusion | flops 4305453056 | bytes 7348224 | tf_op jit(solution)/shard_map/ik,ikh->ih/dot_general | solution.py:52
  343.3 0.0 copy-done
  343.3 0.0 copy-done.2
  343.3 0.0 copy-done.7
  343.3 0.0 copy-start.8
  343.4 0.0 copy-start.9
  343.4 0.0 copy-start.10
  343.4 2.1 multiply_reduce_fusion
  345.5 0.9 multiply_convert_fusion
  346.5 0.0 all-gather.2.cloned.1.call-update
  346.5 0.0 copy-done.8
  346.5 0.0 copy-done.9
  346.6 0.0 copy-done.10
  346.6 0.1 iota_compare_fusion.3
  346.7 1.9 gather_fusion.3
  348.6 1.9 gather_fusion.4
  350.5 0.2 multiply_reduce_fusion.1
  350.7 26.0 %all-gather.2.cloned.1.call-done = bf16[1024,1024]{1,0:T(8,128)(2,1)} async-done(((bf16[256,1024]{1,0:T(8,128)(2,1)}), bf16[1024,1024]{1,0:T(8,128)(2,1)}) %all-gather.2.cloned.1.call-update) | async-done | bytes 2097168 | tf_op jit(solution)/shard_map/all_gather | solution.py:82
  376.7 2.4 fusion.10
  379.2 0.1 reduce_sum.48
  379.3 0.1 copy.45
  379.4 0.7 select_reduce_fusion
  (26 shorter events, 0.3 us)
Async XLA Ops:
  7.2 336.2 %copy-start = (bf16[1024,1024]{1,0:T(8,128)(2,1)S(1)}, bf16[1024,1024]{1,0:T(8,128)(2,1)}, u32[]{:S(2)}) copy-start(bf16[1024,1024]{1,0:T(8,128)(2,1)} %param.20) | copy-start | bytes 6291460
  28.2 17.0 %copy-start.5 = (s32[2]{0:T(128)S(1)}, s32[2]{0:T(128)}, u32[]{:S(2)}) copy-start(s32[2]{0:T(128)} %constant.179) | copy-start | bytes 28
  28.2 47.4 %copy-start.1 = (bf16[256,1024]{1,0:T(8,128)(2,1)S(1)}, bf16[256,1024]{1,0:T(8,128)(2,1)}, u32[]{:S(2)}) copy-start(bf16[256,1024]{1,0:T(8,128)(2,1)} %param.16) | copy-start | bytes 1572868
  101.2 6.2 %copy-start.4 = (s32[2]{0:T(128)S(1)}, s32[2]{0:T(128)}, u32[]{:S(2)}) copy-start(s32[2]{0:T(128)} %param.24) | copy-start | bytes 28
  101.2 8.1 %copy-start.3 = (s32[256,8]{0,1:T(8,128)S(1)}, s32[256,8]{0,1:T(8,128)}, u32[]{:S(2)}) copy-start(s32[256,8]{0,1:T(8,128)} %param.23) | copy-start | bytes 24580
  101.2 191.7 %all-to-all-start.1 = ((bf16[64,64,1024]{2,1,0:T(8,128)(2,1)}), bf16[64,64,1024]{2,1,0:T(8,128)(2,1)}, u32[]{:S(2)}, u32[]{:S(2)}) async-start(bf16[64,64,1024]{2,1,0:T(8,128)(2,1)} %broadcast_select_fusion), calls=%async_computation.1 | async-start | bytes 16777216 | tf_op jit(solution)/shard_map/all_to_all | solution.py:46
  107.1 269.6 %all-gather.2.cloned.1.call-start = ((), (), s32[]{:S(2)}) async-start(), calls=%async_computation.2 | async-start | bytes 2621440 | tf_op jit(solution)/shard_map/all_gather | solution.py:82
  292.9 40.8 %copy-start.6 = (f32[1024]{0:T(1024)S(1)}, f32[1024]{0:T(1024)}, u32[]{:S(2)}) copy-start(f32[1024]{0:T(1024)} %param.18) | copy-start | bytes 12292
  333.7 9.6 %copy-start.2 = (f32[256,1024]{1,0:T(8,128)S(1)}, f32[256,1024]{1,0:T(8,128)}, u32[]{:S(2)}) copy-start(f32[256,1024]{1,0:T(8,128)} %fusion.33) | copy-start | bytes 3145732
  333.7 9.6 %copy-start.7 = (f32[1024]{0:T(1024)S(1)}, f32[1024]{0:T(1024)}, u32[]{:S(2)}) copy-start(f32[1024]{0:T(1024)} %param.21) | copy-start | bytes 12292
  343.3 3.1 copy-start.8
  343.4 3.2 copy-start.9
  343.4 3.2 copy-start.10
Sparse Core Ops, SparseCore 0:
  346.6 30.1 all-gather.1
where the time goes:
time: 388 us; the launch traced here: 387 us
  waiting for transfers between devices  206 us (53%)
  local copies, waits for them, and re-layouts  90.8 us (23%)
  other arithmetic  29.9 us (8%)
  blocking collectives  22.1 us (6%)
  matrix products  17.4 us (4%)
  between operations  14.4 us (4%)
  starting transfers between devices  6.13 us (2%)
    all_to_all x1, waiting for transfers between devices, body(): lax.all_to_all(outgoing, 'shard', split_axis=0, concat_axis=0, tiled=True)  180 us
    gather x1, local copies, waits for them, and re-layouts, body(): gathered = incoming[owners, slot_rank]  40.8 us
    all_gather x1, waiting for transfers between devices, body(): lax.all_gather(embedding, 'region', axis=0, tiled=True)  26 us
    all_to_all x1, blocking collectives, body(): lax.all_to_all(requests, 'shard', split_axis=0, concat_axis=0, tiled=True)  22.1 us
    another operation x3, other arithmetic  18.5 us
    gather x1, local copies, waits for them, and re-layouts, body(): outgoing = jnp.take(features, wanted, axis=0)  18.3 us
    gather x1, local copies, waits for them, and re-layouts, body(): slot_rank = jnp.take_along_axis(before, owners[:, None], axis=1)[:, 0]  16.8 us
    dot_general x1, matrix products, body(): jnp.einsum('ik,ikh->ih', slot_weight.astype(jnp.bfloat16), slot_proj, pre...  9.62 us
  transfers between devices with their start and end apart: 2, of which 2 were waited for; matrix products, arithmetic and copies ran while one was open for 2% of the time, Pallas kernels for 0%

commit v1 on v0

--- a/solution.py
+++ b/solution.py
@@ -6,6 +6,9 @@
 score_scale = 32.0
 margin_value = 1.0
 norm_eps = 1e-06
+_create_side = lambda field_in: jnp.concatenate(
+    jax.lax.all_to_all(jnp.stack(jax.lax.axis_size("region") * [field_in]), "region", 0, 0), axis=0
+)
 
 
 def body(
@@ -77,11 +80,7 @@
     scores = (
         score_scale
         / hidden
-        * jnp.dot(
-            query_emb,
-            lax.all_gather(embedding, "region", axis=0, tiled=True).T,
-            preferred_element_type=jnp.float32,
-        )
+        * jnp.dot(query_emb, _create_side(embedding).T, preferred_element_type=jnp.float32)
     )
     hinge_all = jnp.maximum(scores - positive_score[:, None] + margin_value, 0.0)
     block_mean = jnp.mean(hinge_all.reshape(query_emb.shape[0], -1, block_rows), axis=-1)

time: 388 us -> 376 us (0.969)
  between operations: 14.4 us -> 1.02 us
  starting transfers between devices: 6.13 us -> 10.4 us
    all_gather x1 -> x0, waiting for transfers between devices: 26 us -> none  [body(): lax.all_gather(embedding, 'region', axis=0, tiled=True)]
    all_to_all x0 -> x1, waiting for transfers between devices: none -> 24.9 us  [jax.lax.all_to_all(jnp.stack(jax.lax.axis_size('region') * [field_in]), '...]
    all_to_all x0 -> x1, starting transfers between devices: none -> 4.44 us  [jax.lax.all_to_all(jnp.stack(jax.lax.axis_size('region') * [field_in]), '...]
    unnamed x26 -> x28, local copies, waits for them, and re-layouts: 9.14 us -> 9.15 us
where the time goes in v1:
time: 376 us; the launch traced here: 375 us
  waiting for transfers between devices  205 us (55%)
  local copies, waits for them, and re-layouts  90 us (24%)
  other arithmetic  29.1 us (8%)
  blocking collectives  22.1 us (6%)
  matrix products  17.4 us (5%)
  starting transfers between devices  10.4 us (3%)
    all_to_all x1, waiting for transfers between devices, body(): lax.all_to_all(outgoing, 'shard', split_axis=0, concat_axis=0, tiled=True)  180 us
    gather x1, local copies, waits for them, and re-layouts, body(): gathered = incoming[owners, slot_rank]  40.8 us
    all_to_all x1, waiting for transfers between devices, jax.lax.all_to_all(jnp.stack(jax.lax.axis_size('region') * [field_in]), '...  24.9 us
    all_to_all x1, blocking collectives, body(): lax.all_to_all(requests, 'shard', split_axis=0, concat_axis=0, tiled=True)  22.1 us
    another operation x3, other arithmetic  18.5 us
    gather x1, local copies, waits for them, and re-layouts, body(): outgoing = jnp.take(features, wanted, axis=0)  18.3 us
    gather x1, local copies, waits for them, and re-layouts, body(): slot_rank = jnp.take_along_axis(before, owners[:, None], axis=1)[:, 0]  16.8 us
    dot_general x1, matrix products, body(): jnp.einsum('ik,ikh->ih', slot_weight.astype(jnp.bfloat16), slot_proj, pre...  9.62 us
  transfers between devices with their start and end apart: 2, of which 2 were waited for; matrix products, arithmetic and copies ran while one was open for 2% of the time, Pallas kernels for 0%

profile of v1, /device:TPU:1, one launch (start us, length us, event | category | flops | bytes accessed | tf_op | source)
XLA Modules:
  0.0 375.2 jit_solution(739902140382473218)
XLA Ops:
  0.6 0.0 copy-start
  0.6 1.0 copy.39
  1.6 0.1 reshape.452
  1.7 0.1 reshape.454
  1.8 0.1 reshape.455
  2.0 0.1 reshape.451
  2.1 18.1 %reduce-window.14 = s32[64,16,128]{2,1,0:T(8,128)S(1)} reduce-window(s32[64,16,128]{2,1,0:T(8,128)S(1)} %fusion.15, s32[]{:T(128)} %constant.161.clone.1), window={size=1x1x128 pad=0_0x0_0x127_0}, to_apply=%region_0.1 | reduce-window | flops 16646144 | bytes 1048580 | tf_op jit(solution)/shard_map/reduce-window.3
  20.3 0.2 slice.37
  20.5 0.4 copy.48
  20.9 0.2 reduce-window.15
  21.1 0.2 broadcast_add_fusion
  21.5 0.2 fusion.13
  21.7 0.0 copy-start.6
  21.7 0.0 copy-start.1
  21.7 16.8 %gather_fusion.2 = s32[2048]{0:T(1024)S(1)} fusion(s32[2048,64]{0,1:T(8,128)S(1)} %fusion.13, s32[2048]{0:T(1024)S(1)} %bitcast.56), kind=kCustom, calls=%fused_computation.4 | custom fusion | bytes 32768 | tf_op jit(solution)/shard_map/jit(take_along_axis)/gather | solution.py:45
  38.5 0.1 shift-left_or_fusion
  38.6 0.1 and_reduce_fusion
  38.6 0.0 copy-done.6
  38.6 0.1 multiply_reduce_fusion.2
  38.8 8.1 %scatter_custom_fusion = s32[4096]{0:T(1024)S(1)} fusion(s32[2048]{0:T(1024)S(1)} %broadcast_select_fusion.3, s32[2048]{0:T(1024)S(1)} %get-tuple-element.18, s32[]{:T(128)} %constant.161.clone.1), kind=kCustom, calls=%fused_computation.69 | custom fusion | bytes 16388
  46.8 0.1 all_to_all.16
  46.9 22.1 %all_to_all.25 = s32[64,1,64]{2,1,0:T(1,128)S(1)} all-to-all(s32[64,1,64]{2,1,0:T(1,128)S(1)} %all_to_all.16), channel_id=1, replica_groups=mesh['region'=4,'shard'=64] {'shard'}, dimensions={0} | all-to-all | bytes 32768 | tf_op jit(solution)/shard_map/all_to_all | solution.py:47
  69.0 0.1 reshape.491
  69.1 0.0 copy-done.1
  69.1 18.3 %gather_fusion = bf16[4096,1024]{1,0:T(8,128)(2,1)} fusion(bf16[256,1024]{1,0:T(8,128)(2,1)S(1)} %copy-done.1, s32[4096]{0:T(1024)S(1)} %broadcast_clamp_fusion), kind=kCustom, calls=%fused_computation.2 | custom fusion | bytes 16793600 | tf_op jit(solution)/shard_map/jit(_take)/gather | solution.py:48
  87.4 7.3 %broadcast_select_fusion = bf16[64,64,1024]{2,1,0:T(8,128)(2,1)} fusion(bf16[64,64,1024]{2,1,0:T(8,128)(2,1)} %bitcast.57, pred[64,64]{1,0:T(8,128)(4,1)S(1)} %compare_and_fusion), kind=kLoop, calls=%fused_computation.7 | loop fusion | flops 4194304 | bytes 16781312 | tf_op jit(solution)/shard_map/jit(_take)/select_n | solution.py:48
  94.7 0.0 copy-start.5
  94.7 0.0 copy-start.4
  94.7 5.9 %all-to-all-start.1 = ((bf16[64,64,1024]{2,1,0:T(8,128)(2,1)}), bf16[64,64,1024]{2,1,0:T(8,128)(2,1)}, u32[]{:S(2)}, u32[]{:S(2)}) async-start(bf16[64,64,1024]{2,1,0:T(8,128)(2,1)} %broadcast_select_fusion), calls=%async_computation.1 | async-start | bytes 16777216 | tf_op jit(solution)/shard_map/all_to_all | solution.py:49
  100.6 0.0 copy-done.5
  100.6 0.6 fusion.32
  101.2 1.3 compare_select_fusion.12
  102.5 0.0 copy-done.4
  102.6 0.2 copy.46
  102.7 3.3 fusion.33
  106.0 180.3 %all-to-all-done.1 = bf16[64,64,1024]{2,1,0:T(8,128)(2,1)} async-done(((bf16[64,64,1024]{2,1,0:T(8,128)(2,1)}), bf16[64,64,1024]{2,1,0:T(8,128)(2,1)}, u32[]{:S(2)}, u32[]{:S(2)}) %all-to-all-start.1) | async-done | bytes 8388640 | tf_op jit(solution)/shard_map/all_to_all | solution.py:49
  286.4 0.0 copy-start.7
  286.4 40.8 %gather_fusion.1 = bf16[2048,1024]{1,0:T(8,128)(2,1)} fusion(bf16[64,64,1024]{2,1,0:T(8,128)(2,1)} %all-to-all-done.1, s32[2048]{0:T(1024)S(1)} %bitcast.55), kind=kCustom, calls=%fused_computation.3 | custom fusion | bytes 8404992 | tf_op jit(solution)/shard_map/gather | solution.py:50
  327.2 0.0 copy-done.7
  327.2 9.6 %fusion.1 = f32[256,1,1024]{2,1,0:T(1,128)} fusion(bf16[256,8,1]{1,2,0:T(2,128)(2,1)S(1)} %copy.46, f32[1024]{0:T(1024)S(1)} %copy-done.7, bf16[2048,1024]{1,0:T(8,128)(2,1)} %gather_fusion.1, bf16[1024,1024]{1,0:T(8,128)(2,1)} %param.17), kind=kOutput, calls=%fused_computation.9 | convolution fusion | flops 4305453056 | bytes 7348224 | tf_op jit(solution)/shard_map/ik,ikh->ih/dot_general | solution.py:55
  336.8 0.0 copy-done
  336.8 0.0 copy-done.3
  336.8 0.0 copy-done.8
  336.8 2.1 multiply_reduce_fusion
  338.9 0.0 copy-start.9
  338.9 0.0 copy-start.10
  339.0 0.0 copy-start.11
  339.0 0.1 multiply_convert_fusion
  339.1 0.0 copy-start.2
  339.1 1.6 stack.2
  340.7 4.4 %all-to-all-start.2 = ((bf16[4,256,1024]{2,1,0:T(8,128)(2,1)}), bf16[4,256,1024]{2,1,0:T(8,128)(2,1)}, u32[]{:S(2)}, u32[]{:S(2)}) async-start(bf16[4,256,1024]{2,1,0:T(8,128)(2,1)} %stack.2), calls=%async_computation.2 | async-start | bytes 4194304 | tf_op jit(solution)/shard_map/all_to_all | solution.py:10
  345.1 0.0 copy-done.9
  345.2 0.0 copy-done.10
  345.2 0.0 copy-done.11
  345.2 0.1 iota_compare_fusion.3
  345.3 0.7 gather_fusion.3
  346.0 0.7 gather_fusion.4
  346.7 0.0 copy-done.2
  346.7 0.2 multiply_reduce_fusion.1
  347.0 24.9 %all-to-all-done.2 = bf16[4,256,1024]{2,1,0:T(8,128)(2,1)} async-done(((bf16[4,256,1024]{2,1,0:T(8,128)(2,1)}), bf16[4,256,1024]{2,1,0:T(8,128)(2,1)}, u32[]{:S(2)}, u32[]{:S(2)}) %all-to-all-start.2) | async-done | bytes 2097184 | tf_op jit(solution)/shard_map/all_to_all | solution.py:10
  371.9 2.4 fusion.10
  374.3 0.1 reduce_sum.48
  374.4 0.1 copy.45
  374.5 0.7 select_reduce_fusion
  (28 shorter events, 0.4 us)
Async XLA Ops:
  0.6 336.2 %copy-start = (bf16[1024,1024]{1,0:T(8,128)(2,1)S(1)}, bf16[1024,1024]{1,0:T(8,128)(2,1)}, u32[]{:S(2)}) copy-start(bf16[1024,1024]{1,0:T(8,128)(2,1)} %param.20) | copy-start | bytes 6291460
  21.7 17.0 %copy-start.6 = (s32[2]{0:T(128)S(1)}, s32[2]{0:T(128)}, u32[]{:S(2)}) copy-start(s32[2]{0:T(128)} %constant.179) | copy-start | bytes 28
  21.7 47.4 %copy-start.1 = (bf16[256,1024]{1,0:T(8,128)(2,1)S(1)}, bf16[256,1024]{1,0:T(8,128)(2,1)}, u32[]{:S(2)}) copy-start(bf16[256,1024]{1,0:T(8,128)(2,1)} %param.16) | copy-start | bytes 1572868
  94.7 6.0 %copy-start.5 = (s32[2]{0:T(128)S(1)}, s32[2]{0:T(128)}, u32[]{:S(2)}) copy-start(s32[2]{0:T(128)} %param.24) | copy-start | bytes 28
  94.7 7.9 %copy-start.4 = (s32[256,8]{0,1:T(8,128)S(1)}, s32[256,8]{0,1:T(8,128)}, u32[]{:S(2)}) copy-start(s32[256,8]{0,1:T(8,128)} %param.23) | copy-start | bytes 24580
  94.7 191.7 %all-to-all-start.1 = ((bf16[64,64,1024]{2,1,0:T(8,128)(2,1)}), bf16[64,64,1024]{2,1,0:T(8,128)(2,1)}, u32[]{:S(2)}, u32[]{:S(2)}) async-start(bf16[64,64,1024]{2,1,0:T(8,128)(2,1)} %broadcast_select_fusion), calls=%async_computation.1 | async-start | bytes 16777216 | tf_op jit(solution)/shard_map/all_to_all | solution.py:49
  286.4 40.8 %copy-start.7 = (f32[1024]{0:T(1024)S(1)}, f32[1024]{0:T(1024)}, u32[]{:S(2)}) copy-start(f32[1024]{0:T(1024)} %param.18) | copy-start | bytes 12292
  327.2 9.6 %copy-start.3 = (f32[256,1024]{1,0:T(8,128)S(1)}, f32[256,1024]{1,0:T(8,128)}, u32[]{:S(2)}) copy-start(f32[256,1024]{1,0:T(8,128)} %fusion.33) | copy-start | bytes 3145732
  327.2 9.6 %copy-start.8 = (f32[1024]{0:T(1024)S(1)}, f32[1024]{0:T(1024)}, u32[]{:S(2)}) copy-start(f32[1024]{0:T(1024)} %param.21) | copy-start | bytes 12292
  338.9 6.2 %copy-start.9 = (s32[64]{0:T(128)S(1)}, s32[64]{0:T(128)}, u32[]{:S(2)}) copy-start(s32[64]{0:T(128)} %param.25) | copy-start | bytes 772
  338.9 6.2 %copy-start.10 = (s32[64]{0:T(128)S(1)}, s32[64]{0:T(128)}, u32[]{:S(2)}) copy-start(s32[64]{0:T(128)} %param.26) | copy-start | bytes 772
  339.0 6.3 %copy-start.11 = (s32[1,4]{1,0:T(1,128)S(1)}, s32[1,4]{1,0:T(1,128)}, u32[]{:S(2)}) copy-start(s32[1,4]{1,0:T(1,128)} %param.27) | copy-start | bytes 52
  339.1 7.6 %copy-start.2 = (bf16[256,1024]{1,0:T(8,128)(2,1)}, bf16[256,1024]{1,0:T(8,128)(2,1)S(1)}, u32[]{:S(2)}) copy-start(bf16[256,1024]{1,0:T(8,128)(2,1)S(1)} %multiply_convert_fusion) | copy-start | bytes 1572868
  340.7 31.2 %all-to-all-start.2 = ((bf16[4,256,1024]{2,1,0:T(8,128)(2,1)}), bf16[4,256,1024]{2,1,0:T(8,128)(2,1)}, u32[]{:S(2)}, u32[]{:S(2)}) async-start(bf16[4,256,1024]{2,1,0:T(8,128)(2,1)} %stack.2), calls=%async_computation.2 | async-start | bytes 4194304 | tf_op jit(solution)/shard_map/all_to_all | solution.py:10
